TPU v7x, 128 devices: a whole 4x4x4 slice. The times are simulated.
128 devices in a mesh: blk: 64 (over z, y, x_hi, core), rows: 2 (over x_lo).
Axes of the slice: x: 4 (x_hi: 2, x_lo: 2; x = x_hi * 2 + x_lo), y: 4, z: 4, core: 2. Of those that a mesh axis runs over, the one named last changes fastest.
Arguments:
- panel: bfloat16 [4, 512, 393216], P(None, 'rows', 'blk'), may hold values from -0.009765625 to 0.009765625
- solved: bfloat16 [393216, 1024], P('blk'), may hold values from -6 to 6
- loads: float32 [4, 512, 1024], P(None, 'rows'), may hold values from -6 to 6
- window: bfloat16 [4, 512, 2048], P(None, 'rows'), may hold values from -0.25 to 0.25
- inverses: bfloat16 [4, 512, 512], P(None, 'rows'), as said below
Outputs:
- unknowns: bfloat16 [4, 512, 1024], P(None, 'rows')
Inputs may be any that keep to these rules, and one draw needn't show every extreme that they name: inverses[i] is lower triangular, the inverse of the factor's i-th diagonal block.
All inputs are finite; a program needn't handle non-finite values.
Results may differ from a plain program's by a relative error of at most 0.01.
Values may be sent and summed in bfloat16 or wider, within the bound.
A program may use at most 128 MiB of HBM per device.

v0:
```python
import jax
import jax.numpy as jnp
from jax import lax
from jax.sharding import PartitionSpec as P


def shards(panel, solved, loads, window, inverses):
    partial_value = jnp.einsum("ksc,cr->ksr", panel, solved, preferred_element_type=jnp.float32)
    totals = lax.psum(partial_value, "blk")
    remaining = loads - totals
    block_size = inverses.shape[2]
    step_count = loads.shape[0]
    full_blocks = []
    own_rows = []
    for current in range(step_count):
        residual = remaining[current]
        for earlier in range(current):
            coupling = window[current][:, earlier * block_size : (earlier + 1) * block_size]
            residual = residual - jnp.dot(
                coupling, full_blocks[earlier], preferred_element_type=jnp.float32
            )
        residual = residual.astype(jnp.bfloat16)
        inverse_now = inverses[current]
        solved_part = jnp.dot(
            inverse_now,
            lax.all_gather(residual, "rows", axis=0, tiled=True),
            preferred_element_type=jnp.float32,
        ).astype(jnp.bfloat16)
        own_rows.append(solved_part)
        if current + 1 < step_count:
            full_blocks.append(lax.all_gather(solved_part, "rows", axis=0, tiled=True))
    result = jnp.stack(own_rows)
    return result


def solution(mesh):
    placed = (
        P(None, "rows", "blk"),
        P("blk", None),
        P(None, "rows", None),
        P(None, "rows", None),
        P(None, "rows", None),
    )
    return jax.shard_map(
        shards, mesh=mesh, in_specs=placed, out_specs=P(None, "rows", None), check_vma=False
    )
```

profile of v0, /device:TPU:1, one launch (start us, length us, event | category | flops | bytes accessed | tf_op | source)
XLA Modules:
  0.0 892.1 jit_solution(10524054517992434693)
XLA Ops:
  6.5 19.0 %fusion = f32[4,256,1024]{2,1,0:T(8,128)} fusion(bf16[4,256,6144]{2,1,0:T(8,128)(2,1)} %param.5, bf16[6144,1024]{1,0:T(8,128)(2,1)} %param.6), kind=kOutput, calls=%fused_computation | convolution fusion | flops 12884901888 | bytes 29360128 | tf_op jit(solution)/shard_map/ksc,cr->ksr/dot_general | solution.py:8
  25.6 0.0 all-gather.21.cloned.1.call-start
  25.7 653.3 %all-reduce.2.cloned.1.call-done = f32[4,256,1024]{2,1,0:T(8,128)} async-done(((f32[4,256,1024]{2,1,0:T(8,128)}), f32[4,256,1024]{2,1,0:T(8,128)}) %all-reduce.2.cloned.1.call-update) | async-done | bytes 4194320 | tf_op jit(solution)/shard_map/psum | solution.py:9
  679.0 4.4 sub.21
  683.4 1.9 copy-done
  685.3 0.9 slice.123
  686.2 0.0 all-gather.9.cloned.1.call-start
  686.3 24.5 %all-gather.21.cloned.1.call-done = bf16[1,512,1024]{2,1,0:T(8,128)(2,1)} async-done(((bf16[1,256,1024]{2,1,0:T(8,128)(2,1)}), bf16[1,512,1024]{2,1,0:T(8,128)(2,1)}) %all-gather.21.cloned.1.call-update) | async-done | bytes 1048592 | tf_op jit(solution)/shard_map/all_gather | solution.py:26
  710.7 2.6 convolution_convert_fusion.3
  713.3 0.0 all-gather.11.cloned.1.call-start
  713.4 3.1 slice_bitcast_fusion.3
  716.5 21.7 %all-gather.9.cloned.1.call-done = bf16[512,1024]{0,1:T(8,128)(2,1)} async-done(((bf16[256,1024]{0,1:T(8,128)(2,1)}), bf16[512,1024]{0,1:T(8,128)(2,1)}) %all-gather.9.cloned.1.call-update) | async-done | bytes 1048592 | tf_op jit(solution)/shard_map/all_gather | solution.py:31
  738.2 2.9 fusion.10
  741.1 0.0 all-gather.13.cloned.1.call-start
  741.2 24.9 %all-gather.11.cloned.1.call-done = bf16[512,1024]{1,0:T(8,128)(2,1)} async-done(((bf16[256,1024]{1,0:T(8,128)(2,1)}), bf16[512,1024]{1,0:T(8,128)(2,1)}) %all-gather.11.cloned.1.call-update) | async-done | bytes 1048592 | tf_op jit(solution)/shard_map/all_gather | solution.py:26
  766.1 2.6 convolution_convert_fusion.2
  768.6 0.0 all-gather.15.cloned.1.call-start
  768.7 24.8 %all-gather.13.cloned.1.call-done = bf16[512,1024]{0,1:T(8,128)(2,1)} async-done(((bf16[256,1024]{0,1:T(8,128)(2,1)}), bf16[512,1024]{0,1:T(8,128)(2,1)}) %all-gather.13.cloned.1.call-update) | async-done | bytes 1048592 | tf_op jit(solution)/shard_map/all_gather | solution.py:31
  793.5 1.8 convolution_bitcast_fusion.3
  795.3 2.5 fusion.9
  797.8 0.0 all-gather.17.cloned.1.call-start
  797.9 24.9 %all-gather.15.cloned.1.call-done = bf16[512,1024]{1,0:T(8,128)(2,1)} async-done(((bf16[256,1024]{1,0:T(8,128)(2,1)}), bf16[512,1024]{1,0:T(8,128)(2,1)}) %all-gather.15.cloned.1.call-update) | async-done | bytes 1048592 | tf_op jit(solution)/shard_map/all_gather | solution.py:26
  822.7 2.5 convolution_convert_fusion.1
  825.3 0.0 all-gather.19.cloned.1.call-start
  825.4 1.4 convolution_bitcast_fusion.1
  826.8 23.4 %all-gather.17.cloned.1.call-done = bf16[512,1024]{0,1:T(8,128)(2,1)} async-done(((bf16[256,1024]{0,1:T(8,128)(2,1)}), bf16[512,1024]{0,1:T(8,128)(2,1)}) %all-gather.17.cloned.1.call-update) | async-done | bytes 1048592 | tf_op jit(solution)/shard_map/all_gather | solution.py:31
  850.2 1.7 convolution_bitcast_fusion
  851.9 2.6 fusion.8
  854.5 24.9 %all-gather.19.cloned.1.call-done = bf16[512,1024]{1,0:T(8,128)(2,1)} async-done(((bf16[256,1024]{1,0:T(8,128)(2,1)}), bf16[512,1024]{1,0:T(8,128)(2,1)}) %all-gather.19.cloned.1.call-update) | async-done | bytes 1048592 | tf_op jit(solution)/shard_map/all_gather | solution.py:26
  879.5 1.7 fusion.11
  881.2 1.6 pad_maximum_fusion
  882.8 2.4 copy.6
  (14 shorter events, 0.1 us)
Async XLA Ops:
  6.5 672.4 %all-reduce.2.cloned.1.call-start = ((), (), s32[]{:S(2)}) async-start(), calls=%async_computation | async-start | bytes 8388608 | tf_op jit(solution)/shard_map/psum | solution.py:9
  25.6 685.1 %all-gather.21.cloned.1.call-start = ((), (), s32[]{:S(2)}) async-start(), calls=%async_computation.7 | async-start | bytes 1572864 | tf_op jit(solution)/shard_map/all_gather | solution.py:26
  683.4 1.9 copy-start
  686.2 52.0 %all-gather.9.cloned.1.call-start = ((), (), s32[]{:S(2)}) async-start(), calls=%async_computation.1 | async-start | bytes 1572864 | tf_op jit(solution)/shard_map/all_gather | solution.py:31
  713.3 52.7 %all-gather.11.cloned.1.call-start = ((), (), s32[]{:S(2)}) async-start(), calls=%async_computation.2 | async-start | bytes 1572864 | tf_op jit(solution)/shard_map/all_gather | solution.py:26
  738.2 57.1 %copy-start.1 = (bf16[512,1024]{0,1:T(8,128)(2,1)S(1)}, bf16[512,1024]{0,1:T(8,128)(2,1)}, u32[]{:S(2)}) copy-start(bf16[512,1024]{0,1:T(8,128)(2,1)} %all-gather.9.cloned.1.call-done) | copy-start | bytes 3145732
  741.1 52.4 %all-gather.13.cloned.1.call-start = ((), (), s32[]{:S(2)}) async-start(), calls=%async_computation.3 | async-start | bytes 1572864 | tf_op jit(solution)/shard_map/all_gather | solution.py:31
  768.6 54.1 %all-gather.15.cloned.1.call-start = ((), (), s32[]{:S(2)}) async-start(), calls=%async_computation.4 | async-start | bytes 1572864 | tf_op jit(solution)/shard_map/all_gather | solution.py:26
  793.5 31.8 %copy-start.2 = (bf16[512,1024]{0,1:T(8,128)(2,1)S(1)}, bf16[512,1024]{0,1:T(8,128)(2,1)}, u32[]{:S(2)}) copy-start(bf16[512,1024]{0,1:T(8,128)(2,1)} %all-gather.13.cloned.1.call-done) | copy-start | bytes 3145732
  797.8 52.4 %all-gather.17.cloned.1.call-start = ((), (), s32[]{:S(2)}) async-start(), calls=%async_computation.5 | async-start | bytes 1572864 | tf_op jit(solution)/shard_map/all_gather | solution.py:31
  825.3 54.2 %all-gather.19.cloned.1.call-start = ((), (), s32[]{:S(2)}) async-start(), calls=%async_computation.6 | async-start | bytes 1572864 | tf_op jit(solution)/shard_map/all_gather | solution.py:26
Sparse Core Ops, SparseCore 0:
  25.7 653.1 all-reduce.1
  686.3 24.3 all-gather.20
  713.4 24.7 all-gather.8
  741.3 24.7 all-gather.10
  768.8 24.7 all-gather.12
  797.9 24.7 all-gather.14
  825.4 24.7 all-gather.16
  854.7 24.7 all-gather.18
where the time goes:
time: 892 us
  waiting for transfers between devices  823 us (92%)
  matrix products  41.4 us (5%)
  between operations  13.6 us (2%)
    psum x1, waiting for transfers between devices, shards(): totals = lax.psum(partial_value, 'blk')  653 us
    all_gather x4, waiting for transfers between devices, shards(): lax.all_gather(residual, 'rows', axis=0, tiled=True)  99.1 us
    all_gather x3, waiting for transfers between devices, shards(): full_blocks.append(lax.all_gather(solved_part, 'rows', axis=0, tiled=True))  69.9 us
    dot_general x1, matrix products, shards(): jnp.einsum('ksc,cr->ksr', panel, solved, preferred_element_type=jnp.float32)  19 us
  transfers between devices with their start and end apart: 8, of which 8 were waited for; matrix products, arithmetic and copies ran while one was open for 1% of the time, Pallas kernels for 0%

commit v1 on v0

--- a/solution.py
+++ b/solution.py
@@ -23,7 +23,12 @@
         inverse_now = inverses[current]
         solved_part = jnp.dot(
             inverse_now,
-            lax.all_gather(residual, "rows", axis=0, tiled=True),
+            jnp.concatenate(
+                lax.all_to_all(
+                    jnp.stack([residual for _ in range(lax.axis_size("rows"))], 0), "rows", 0, 0
+                ),
+                0,
+            ),
             preferred_element_type=jnp.float32,
         ).astype(jnp.bfloat16)
         own_rows.append(solved_part)

time: 892 us -> 851 us (0.954)
  waiting for transfers between devices: 823 us -> 725 us
  blocking collectives: 0 us -> 61.3 us
    all_gather x4 -> x0, waiting for transfers between devices: 99.1 us -> none  [shards(): lax.all_gather(residual, 'rows', axis=0, tiled=True)]
    all_to_all x0 -> x4, blocking collectives: none -> 61.3 us  [shards(): lax.all_to_all(jnp.stack([residual for _ in range(lax.axis_size('rows'))]...]
  transfers between devices with their start and end apart: 8 -> 4, of which waited for: 8 -> 4; matrix products, arithmetic and copies ran while one was open for 1% -> 1% of each run, Pallas kernels for 0% -> 0%
where the time goes in v1:
time: 851 us; the launch traced here: 850 us
  waiting for transfers between devices  725 us (85%)
  blocking collectives  61.3 us (7%)
  matrix products  37.7 us (4%)
  between operations  13.3 us (2%)
    psum x1, waiting for transfers between devices, shards(): totals = lax.psum(partial_value, 'blk')  653 us
    all_gather x3, waiting for transfers between devices, shards(): full_blocks.append(lax.all_gather(solved_part, 'rows', axis=0, tiled=True))  71.7 us
    all_to_all x4, blocking collectives, shards(): lax.all_to_all(jnp.stack([residual for _ in range(lax.axis_size('rows'))]...  61.3 us
    dot_general x1, matrix products, shards(): jnp.einsum('ksc,cr->ksr', panel, solved, preferred_element_type=jnp.float32)  19 us
  transfers between devices with their start and end apart: 4, of which 4 were waited for; matrix products, arithmetic and copies ran while one was open for 1% of the time, Pallas kernels for 0%

profile of v1, /device:TPU:1, one launch (start us, length us, event | category | flops | bytes accessed | tf_op | source)
XLA Modules:
  0.0 850.0 jit_solution(10565429064364186751)
XLA Ops:
  6.5 19.0 %fusion = f32[4,256,1024]{2,1,0:T(8,128)} fusion(bf16[4,256,6144]{2,1,0:T(8,128)(2,1)} %param.5, bf16[6144,1024]{1,0:T(8,128)(2,1)} %param.6), kind=kOutput, calls=%fused_computation | convolution fusion | flops 12884901888 | bytes 29360128 | tf_op jit(solution)/shard_map/ksc,cr->ksr/dot_general | solution.py:8
  25.6 0.0 all-gather.4.cloned.1.call-start
  25.6 653.3 %all-reduce.2.cloned.1.call-done = f32[4,256,1024]{2,1,0:T(8,128)} async-done(((f32[4,256,1024]{2,1,0:T(8,128)}), f32[4,256,1024]{2,1,0:T(8,128)}) %all-reduce.2.cloned.1.call-update) | async-done | bytes 4194320 | tf_op jit(solution)/shard_map/psum | solution.py:9
  678.9 4.4 sub.21
  683.4 2.0 copy-done
  685.3 0.1 slice.123
  685.4 0.1 pad_maximum_fusion.1
  685.5 15.2 %all_to_all.20 = bf16[2,256,1024]{2,1,0:T(8,128)(2,1)S(1)} all-to-all(bf16[2,256,1024]{2,1,0:T(8,128)(2,1)S(1)} %pad_maximum_fusion.1), channel_id=1, replica_groups=mesh['blk'=64,'rows'=2] {'rows'}, dimensions={0} | all-to-all | bytes 2097152 | tf_op jit(solution)/shard_map/all_to_all | solution.py:27
  700.7 2.2 convolution_convert_fusion.3
  703.0 0.0 all-gather.6.cloned.1.call-start
  703.0 3.1 slice_bitcast_fusion.3
  706.1 21.7 %all-gather.4.cloned.1.call-done = bf16[512,1024]{0,1:T(8,128)(2,1)} async-done(((bf16[256,1024]{0,1:T(8,128)(2,1)}), bf16[512,1024]{0,1:T(8,128)(2,1)}) %all-gather.4.cloned.1.call-update) | async-done | bytes 1048592 | tf_op jit(solution)/shard_map/all_gather | solution.py:36
  727.8 2.0 fusion.11
  729.8 0.1 pad_maximum_fusion.2
  729.9 15.4 %all_to_all.21 = bf16[2,256,1024]{2,1,0:T(8,128)(2,1)S(1)} all-to-all(bf16[2,256,1024]{2,1,0:T(8,128)(2,1)S(1)} %pad_maximum_fusion.2), channel_id=1, replica_groups=mesh['blk'=64,'rows'=2] {'rows'}, dimensions={0} | all-to-all | bytes 2097152 | tf_op jit(solution)/shard_map/all_to_all | solution.py:27
  745.4 2.2 convolution_convert_fusion.2
  747.6 0.0 all-gather.8.cloned.1.call-start
  747.7 25.7 %all-gather.6.cloned.1.call-done = bf16[512,1024]{0,1:T(8,128)(2,1)} async-done(((bf16[256,1024]{0,1:T(8,128)(2,1)}), bf16[512,1024]{0,1:T(8,128)(2,1)}) %all-gather.6.cloned.1.call-update) | async-done | bytes 1048592 | tf_op jit(solution)/shard_map/all_gather | solution.py:36
  773.4 1.7 convolution_bitcast_fusion.3
  775.1 1.8 fusion.12
  776.9 0.1 pad_maximum_fusion.3
  777.0 15.3 %all_to_all.22 = bf16[2,256,1024]{2,1,0:T(8,128)(2,1)S(1)} all-to-all(bf16[2,256,1024]{2,1,0:T(8,128)(2,1)S(1)} %pad_maximum_fusion.3), channel_id=1, replica_groups=mesh['blk'=64,'rows'=2] {'rows'}, dimensions={0} | all-to-all | bytes 2097152 | tf_op jit(solution)/shard_map/all_to_all | solution.py:27
  792.3 2.2 convolution_convert_fusion.1
  794.5 1.4 convolution_bitcast_fusion.1
  796.0 24.3 %all-gather.8.cloned.1.call-done = bf16[512,1024]{0,1:T(8,128)(2,1)} async-done(((bf16[256,1024]{0,1:T(8,128)(2,1)}), bf16[512,1024]{0,1:T(8,128)(2,1)}) %all-gather.8.cloned.1.call-update) | async-done | bytes 1048592 | tf_op jit(solution)/shard_map/all_gather | solution.py:36
  820.3 1.7 convolution_bitcast_fusion
  822.0 1.9 fusion.13
  823.9 0.1 pad_maximum_fusion.4
  824.0 15.3 %all_to_all.23 = bf16[2,256,1024]{2,1,0:T(8,128)(2,1)S(1)} all-to-all(bf16[2,256,1024]{2,1,0:T(8,128)(2,1)S(1)} %pad_maximum_fusion.4), channel_id=1, replica_groups=mesh['blk'=64,'rows'=2] {'rows'}, dimensions={0} | all-to-all | bytes 2097152 | tf_op jit(solution)/shard_map/all_to_all | solution.py:27
  839.3 1.4 fusion.14
  840.8 0.3 pad_maximum_fusion
  841.1 2.4 copy.12
  (16 shorter events, 0.1 us)
Async XLA Ops:
  6.5 672.4 %all-reduce.2.cloned.1.call-start = ((), (), s32[]{:S(2)}) async-start(), calls=%async_computation.4 | async-start | bytes 8388608 | tf_op jit(solution)/shard_map/psum | solution.py:9
  25.6 702.2 %all-gather.4.cloned.1.call-start = ((), (), s32[]{:S(2)}) async-start(), calls=%async_computation.5 | async-start | bytes 1572864 | tf_op jit(solution)/shard_map/all_gather | solution.py:36
  683.3 2.0 copy-start
  703.0 70.4 %all-gather.6.cloned.1.call-start = ((), (), s32[]{:S(2)}) async-start(), calls=%async_computation.6 | async-start | bytes 1572864 | tf_op jit(solution)/shard_map/all_gather | solution.py:36
  729.8 45.2 %copy-start.1 = (bf16[512,1024]{0,1:T(8,128)(2,1)S(1)}, bf16[512,1024]{0,1:T(8,128)(2,1)}, u32[]{:S(2)}) copy-start(bf16[512,1024]{0,1:T(8,128)(2,1)} %all-gather.4.cloned.1.call-done) | copy-start | bytes 3145732
  747.6 72.7 %all-gather.8.cloned.1.call-start = ((), (), s32[]{:S(2)}) async-start(), calls=%async_computation.7 | async-start | bytes 1572864 | tf_op jit(solution)/shard_map/all_gather | solution.py:36
  775.1 19.5 %copy-start.2 = (bf16[512,1024]{0,1:T(8,128)(2,1)S(1)}, bf16[512,1024]{0,1:T(8,128)(2,1)}, u32[]{:S(2)}) copy-start(bf16[512,1024]{0,1:T(8,128)(2,1)} %all-gather.6.cloned.1.call-done) | copy-start | bytes 3145732
  822.0 18.8 %copy-start.3 = (bf16[1024,256]{1,0:T(8,128)(2,1)S(1)}, bf16[1024,256]{1,0:T(8,128)(2,1)}, u32[]{:S(2)}) copy-start(bf16[1024,256]{1,0:T(8,128)(2,1)} %convolution_convert_fusion.3) | copy-start | bytes 1572868
  822.0 18.8 %copy-start.4 = (bf16[1024,256]{1,0:T(8,128)(2,1)S(1)}, bf16[1024,256]{1,0:T(8,128)(2,1)}, u32[]{:S(2)}) copy-start(bf16[1024,256]{1,0:T(8,128)(2,1)} %convolution_convert_fusion.2) | copy-start | bytes 1572868
  822.0 18.8 %copy-start.5 = (bf16[1024,256]{1,0:T(8,128)(2,1)S(1)}, bf16[1024,256]{1,0:T(8,128)(2,1)}, u32[]{:S(2)}) copy-start(bf16[1024,256]{1,0:T(8,128)(2,1)} %convolution_convert_fusion.1) | copy-start | bytes 1572868
Sparse Core Ops, SparseCore 0:
  25.7 653.1 all-reduce.1
  703.1 24.6 all-gather.3
  747.7 25.5 all-gather.5
  794.7 25.5 all-gather.7
